TPU v7x, 32 devices: a whole 2x2x4 slice. The times are simulated.
32 devices in a mesh: curve: 8 (over z, y), band: 4 (over x, core).
Axes of the slice: x: 2, y: 2, z: 4, core: 2. Of those that a mesh axis runs over, the one named last changes fastest.
Arguments:
- state: float32 [16, 2048, 128], P('band', 'curve'), may hold values from -3 to 3
- blocks: bfloat16 [2048, 4, 128, 128], P('curve', 'band'), may hold values from -0.25 to 0.25
- diag_blocks: bfloat16 [2048, 128, 128], P(('curve', 'band')), may hold values from -1 to 1, as said below
- block_cols: int32 [2048, 4], P('curve', 'band'), may hold values from 0 to 2047, as said below
Outputs:
- updated: float32 [16, 2048, 128], P('band', 'curve')
Inputs may be any that keep to these rules, and one draw needn't show every extreme that they name: `diag_blocks`: every diagonal block is symmetric. `block_cols`: A column is never the row's own patch, and no pair of patches is stored twice, in either order. The owner of patch p is index p // 256 of curve. Of the 256 rows of one index of curve, in each slot exactly 8 have their column on another index: 2 on each of 4 other indices; the columns of the others lie on the own index.
All inputs are finite; a program needn't handle non-finite values.
Results may differ from a plain program's by a relative error of at most 0.0003.
The roundings to bfloat16 on the way count: a program that leaves them out, or rounds other values in their place, can miss the bound.
Values may be sent and summed in bfloat16 or wider, within the bound.
No kernel may reach another device: no remote copies, remote signals or barrier semaphores. Data moves between devices by JAX's collectives and lax.ppermute only.
A program may use at most 64 MiB of HBM per device.

v0:
```python
import jax
import jax.numpy as jnp
from jax import lax
from jax.sharding import PartitionSpec as P

CAP = 2
TAYLOR = 16
epsilon = 1e-06
time_step = 0.5
quadratic = 1.0


def nonlinear(field):
    return quadratic * field * field - field * field * field


def phi_weights(alpha_first, beta_first, alpha_second):

    def advance(turn, carry):
        term_one, term_two, total_one, total_two = carry
        factor = time_step / (turn + 1.0)
        next_one = factor * (alpha_first * term_one + beta_first * term_two)
        next_two = factor * (beta_first * term_one + alpha_second * term_two)
        return (next_one, next_two, total_one + next_one, total_two + next_two)

    ones = jnp.ones_like(alpha_first)
    zeros = jnp.zeros_like(alpha_first)
    result = lax.fori_loop(1, TAYLOR, advance, (ones, zeros, ones, zeros))
    return (result[2], result[3])


def routing(block_cols):
    groups = lax.axis_size("curve")
    here = lax.axis_index("curve")
    patch_rows = block_cols.shape[0]
    columns = block_cols[:, 0]
    owner = columns // patch_rows
    target = columns % patch_rows
    remote = owner != here
    peers = jnp.arange(groups, dtype=jnp.int32)
    member = ((owner[:, None] == peers[None, :]) & remote[:, None]).astype(jnp.int32)
    rank = jnp.sum(jnp.cumsum(member, axis=0) * member, axis=1) - 1
    bucket = jnp.where(remote, owner * CAP + rank, groups * CAP)
    pick = jnp.where(remote, patch_rows + owner * CAP + rank, target)
    wanted = jnp.full((groups * CAP + 1,), -1, jnp.int32).at[bucket].set(target)
    asked = lax.all_to_all(
        wanted[:-1].reshape(groups, CAP), "curve", split_axis=0, concat_axis=0, tiled=True
    )
    asked_flat = asked.reshape(-1)
    return (remote, target, bucket, pick, jnp.maximum(asked_flat, 0), asked_flat >= 0)


def local_product(whole, blocks, diag_blocks, plan):
    remote, target, bucket, pick, asked_index, asked_valid = plan
    groups = lax.axis_size("curve")
    vectors, patch_rows, node_count = whole.shape
    reply = whole[:, asked_index, :].reshape(vectors, groups, CAP, node_count)
    arrived = lax.all_to_all(reply, "curve", split_axis=1, concat_axis=1, tiled=True)
    pool = jnp.concatenate([whole, arrived.reshape(vectors, groups * CAP, node_count)], axis=1)
    gathered = pool[:, pick, :]
    stored = blocks[:, 0]
    result = jnp.einsum("rac,vrc->vra", stored, gathered, preferred_element_type=jnp.float32)
    mirrored = jnp.einsum("rac,vra->vrc", stored, whole, preferred_element_type=jnp.float32)
    kept = jnp.where(remote[None, :, None], 0.0, mirrored)
    result = result.at[:, target, :].add(kept)
    outgoing = (
        jnp.zeros((vectors, groups * CAP + 1, node_count), jnp.float32)
        .at[:, bucket, :]
        .add(mirrored)
    )
    outgoing = outgoing[:, :-1, :].reshape(vectors, groups, CAP, node_count)
    returned = lax.all_to_all(outgoing, "curve", split_axis=1, concat_axis=1, tiled=True)
    returned = jnp.where(
        asked_valid[None, :, None], returned.reshape(vectors, groups * CAP, node_count), 0.0
    )
    result = result.at[:, asked_index, :].add(returned)
    quarter = diag_blocks.shape[0]
    start = lax.axis_index("band") * quarter
    own_rows = lax.dynamic_slice_in_dim(whole, start, quarter, 1)
    diagonal = jnp.einsum("rac,vrc->vra", diag_blocks, own_rows, preferred_element_type=jnp.float32)
    current = lax.dynamic_slice_in_dim(result, start, quarter, 1)
    return lax.dynamic_update_slice_in_dim(result, current + diagonal, start, 1)


def operate(vector, blocks, diag_blocks, plan):
    whole = lax.all_gather(vector, "band", axis=0, tiled=True)
    product = lax.psum_scatter(
        local_product(whole, blocks, diag_blocks, plan), "band", scatter_dimension=0, tiled=True
    )
    return product


def body(state, blocks, diag_blocks, block_cols):
    plan = routing(block_cols)
    drive = operate(state.astype(jnp.bfloat16), blocks, diag_blocks, plan) + nonlinear(state)
    drive_norm = lax.psum(jnp.sum(drive * drive, axis=(1, 2)), "curve")
    beta_zero = jnp.sqrt(drive_norm + epsilon)
    first = drive / beta_zero[:, None, None]
    image = operate(first.astype(jnp.bfloat16), blocks, diag_blocks, plan)
    alpha_first, energy = lax.psum(
        (jnp.sum(first * image, axis=(1, 2)), jnp.sum(image * image, axis=(1, 2))), "curve"
    )
    rest = image - alpha_first[:, None, None] * first
    beta_first = jnp.sqrt(jnp.maximum(energy - alpha_first * alpha_first, 0.0) + epsilon)
    second = rest / beta_first[:, None, None]
    image_second = operate(second.astype(jnp.bfloat16), blocks, diag_blocks, plan)
    image_second = image_second - beta_first[:, None, None] * first
    alpha_second = lax.psum(jnp.sum(second * image_second, axis=(1, 2)), "curve")
    weight_one, weight_two = phi_weights(alpha_first, beta_first, alpha_second)
    combined = weight_one[:, None, None] * first + weight_two[:, None, None] * second
    updated = state + time_step * beta_zero[:, None, None] * combined
    return updated


def solution(mesh):
    return jax.shard_map(
        body,
        mesh=mesh,
        in_specs=(
            P("band", "curve", None),
            P("curve", "band", None, None),
            P(("curve", "band"), None, None),
            P("curve", "band"),
        ),
        out_specs=P("band", "curve", None),
        check_vma=False,
    )
```

profile of v0, /device:TPU:0, one launch (start us, length us, event | category | flops | bytes accessed | tf_op | source)
XLA Modules:
  0.0 534.8 jit_solution(13686195170682434651)
XLA Ops:
  6.5 1.9 convert_element_type.21
  13.6 7.3 %all-to-all-start = ((s32[8,1,2]{2,1,0:T(1,128)}), s32[8,1,2]{2,1,0:T(1,128)S(1)}, u32[]{:S(2)}, u32[]{:S(2)}) async-start(s32[8,1,2]{2,1,0:T(1,128)} %bitcast.7), calls=%async_computation | async-start | bytes 8192 | tf_op jit(solution)/shard_map/all_to_all | solution.py:46
  21.6 5.8 %all-to-all-done = s32[8,1,2]{2,1,0:T(1,128)S(1)} async-done(((s32[8,1,2]{2,1,0:T(1,128)}), s32[8,1,2]{2,1,0:T(1,128)S(1)}, u32[]{:S(2)}, u32[]{:S(2)}) %all-to-all-start) | async-done | bytes 96 | tf_op jit(solution)/shard_map/all_to_all | solution.py:46
  31.4 5.5 %all-to-all-start.1 = ((bf16[16,8,2,128]{3,0,2,1:T(8,128)(2,1)}), bf16[16,8,2,128]{3,0,2,1:T(8,128)(2,1)S(1)}, u32[]{:S(2)}, u32[]{:S(2)}) async-start(bf16[16,8,2,128]{3,0,2,1:T(8,128)(2,1)} %bitcast.9), calls=%async_computation.1 | async-start | bytes 131072 | tf_op jit(solution)/shard_map/all_to_all | solution.py:58
  37.0 8.0 %broadcast_select_fusion.6 = (f32[256,16,128]{2,1,0:T(8,128)}, f32[256,16,128]{2,1,0:T(8,128)}) fusion(pred[256]{0:T(512)(128)(4,1)S(1)} %fusion.43, bf16[256,1,128,128]{3,2,1,0:T(8,128)(2,1)} %param.7, bf16[16,256,128]{2,1,0:T(8,128)(2,1)} %all-gather.4.cloned.1.call-done), kind=kOutput, calls=%fused_computation.56 | convolution fusion | flops 134742016 | bytes 13631744 | tf_op jit(solution)/shard_map/rac,vra->vrc/dot_general | solution.py:63
  45.0 20.9 %scatter_fusion.1 = f32[16,17,128]{2,0,1:T(8,128)S(1)} fusion(f32[16,17,128]{2,0,1:T(8,128)S(1)} %broadcast.192.clone, s32[256]{0:T(256)S(1)} %bitcast.116, f32[256,16,128]{2,1,0:T(8,128)} %get-tuple-element.211), kind=kCustom, calls=%fused_computation.8 | custom fusion | flops 524288 | bytes 6292480 | tf_op jit(solution)/shard_map/scatter-add | solution.py:69
  66.6 6.0 %all-to-all-start.2 = ((f32[16,8,2,128]{3,0,2,1:T(8,128)}), f32[16,8,2,128]{3,0,2,1:T(8,128)S(1)}, u32[]{:S(2)}, u32[]{:S(2)}) async-start(f32[16,8,2,128]{3,0,2,1:T(8,128)} %bitcast.16), calls=%async_computation.2 | async-start | bytes 262144 | tf_op jit(solution)/shard_map/all_to_all | solution.py:72
  73.7 3.0 gather_fusion.1
  76.7 9.5 %fusion.14 = f32[16,256,128]{2,0,1:T(8,128)} fusion(bf16[256,1,128,128]{3,2,1,0:T(8,128)(2,1)} %param.7, bf16[256,16,128]{2,1,0:T(8,128)(2,1)} %gather_fusion.1), kind=kOutput, calls=%fused_computation.36 | convolution fusion | flops 134217728 | bytes 11534336 | tf_op jit(solution)/shard_map/rac,vrc->vra/dot_general | solution.py:62
  86.2 31.4 %scatter_fusion = f32[16,256,128]{2,0,1:T(8,128)} fusion(f32[16,256,128]{2,0,1:T(8,128)} %fusion.14, s32[256]{0:T(256)S(1)} %bitcast.112, f32[256,16,128]{2,1,0:T(8,128)} %get-tuple-element.210), kind=kCustom, calls=%fused_computation.7 | custom fusion | flops 524288 | bytes 6292480 | tf_op jit(solution)/shard_map/scatter-add | solution.py:65
  117.7 2.5 scatter_fusion.2
  120.3 3.0 fusion.24
  123.3 3.6 copy.35
  127.0 31.7 %reduce-scatter.4.cloned.1.call-done = f32[4,256,128]{2,1,0:T(8,128)} async-done(((f32[16,256,128]{2,1,0:T(8,128)}), f32[4,256,128]{2,1,0:T(8,128)}) %reduce-scatter.4.cloned.1.call-update) | async-done | bytes 524304 | tf_op jit(solution)/shard_map/reduce_scatter | solution.py:87
  160.0 21.3 %psum.28 = f32[4]{0:T(128)S(1)} all-reduce(f32[4]{0:T(128)S(1)} %multiply_reduce_fusion.3), channel_id=1, replica_groups=mesh['curve'=8,'band'=4] {'curve'}, use_global_device_ids=true, to_apply=%region_9.10 | all-reduce | flops 4 | bytes 32 | tf_op jit(solution)/shard_map/psum | solution.py:96
  183.3 13.2 %all-gather.6.cloned.1.call-done = bf16[16,256,128]{2,1,0:T(8,128)(2,1)} async-done(((bf16[4,256,128]{2,1,0:T(8,128)(2,1)}), bf16[16,256,128]{2,1,0:T(8,128)(2,1)}) %all-gather.6.cloned.1.call-update) | async-done | bytes 1048592 | tf_op jit(solution)/shard_map/all_gather | solution.py:86
  196.5 2.9 copy.37
  199.3 2.4 gather_fusion.2
  201.7 5.5 %all-to-all-start.3 = ((bf16[16,8,2,128]{3,0,2,1:T(8,128)(2,1)}), bf16[16,8,2,128]{3,0,2,1:T(8,128)(2,1)S(1)}, u32[]{:S(2)}, u32[]{:S(2)}) async-start(bf16[16,8,2,128]{3,0,2,1:T(8,128)(2,1)} %bitcast.21), calls=%async_computation.4 | async-start | bytes 131072 | tf_op jit(solution)/shard_map/all_to_all | solution.py:58
  207.3 8.0 %broadcast_select_fusion.5 = (f32[256,16,128]{2,1,0:T(8,128)}, f32[256,16,128]{2,1,0:T(8,128)}) fusion(pred[256]{0:T(512)(128)(4,1)S(1)} %fusion.43, bf16[256,1,128,128]{3,2,1,0:T(8,128)(2,1)} %param.7, bf16[16,256,128]{2,1,0:T(8,128)(2,1)} %all-gather.6.cloned.1.call-done), kind=kOutput, calls=%fused_computation.55 | convolution fusion | flops 134742016 | bytes 13631744 | tf_op jit(solution)/shard_map/rac,vra->vrc/dot_general | solution.py:63
  215.3 20.9 %scatter_fusion.4 = f32[16,17,128]{2,0,1:T(8,128)S(1)} fusion(f32[16,17,128]{2,0,1:T(8,128)S(1)} %broadcast.192.clone.1, s32[256]{0:T(256)S(1)} %bitcast.117, f32[256,16,128]{2,1,0:T(8,128)} %get-tuple-element.213), kind=kCustom, calls=%fused_computation.11 | custom fusion | flops 524288 | bytes 6292480 | tf_op jit(solution)/shard_map/scatter-add | solution.py:69
  236.9 6.0 %all-to-all-start.4 = ((f32[16,8,2,128]{3,0,2,1:T(8,128)}), f32[16,8,2,128]{3,0,2,1:T(8,128)S(1)}, u32[]{:S(2)}, u32[]{:S(2)}) async-start(f32[16,8,2,128]{3,0,2,1:T(8,128)} %bitcast.25), calls=%async_computation.5 | async-start | bytes 262144 | tf_op jit(solution)/shard_map/all_to_all | solution.py:72
  242.9 2.3 pad_maximum_fusion.1
  245.3 3.0 gather_fusion.3
  248.3 9.5 %fusion.17 = f32[16,256,128]{2,0,1:T(8,128)} fusion(bf16[256,1,128,128]{3,2,1,0:T(8,128)(2,1)} %param.7, bf16[256,16,128]{2,1,0:T(8,128)(2,1)} %gather_fusion.3), kind=kOutput, calls=%fused_computation.37 | convolution fusion | flops 134217728 | bytes 11534336 | tf_op jit(solution)/shard_map/rac,vrc->vra/dot_general | solution.py:62
  257.8 31.4 %scatter_fusion.3 = f32[16,256,128]{2,0,1:T(8,128)} fusion(f32[16,256,128]{2,0,1:T(8,128)} %fusion.17, s32[256]{0:T(256)S(1)} %bitcast.113, f32[256,16,128]{2,1,0:T(8,128)} %get-tuple-element.212), kind=kCustom, calls=%fused_computation.10 | custom fusion | flops 524288 | bytes 6292480 | tf_op jit(solution)/shard_map/scatter-add | solution.py:65
  289.3 2.5 scatter_fusion.5
  291.8 3.1 fusion.26
  295.0 3.6 copy.40
  298.7 31.7 %reduce-scatter.6.cloned.1.call-done = f32[4,256,128]{2,1,0:T(8,128)} async-done(((f32[16,256,128]{2,1,0:T(8,128)}), f32[4,256,128]{2,1,0:T(8,128)}) %reduce-scatter.6.cloned.1.call-update) | async-done | bytes 524304 | tf_op jit(solution)/shard_map/reduce_scatter | solution.py:87
  331.6 21.3 %all-reduce = (f32[4]{0:T(128)S(1)}, f32[4]{0:T(128)S(1)}) all-reduce(f32[4]{0:T(128)S(1)} %get-tuple-element.175, f32[4]{0:T(128)S(1)} %get-tuple-element.174), channel_id=1, replica_groups=mesh['curve'=8,'band'=4] {'curve'}, use_global_device_ids=true, to_apply=%region_15.16 | all-reduce | flops 8 | bytes 64 | tf_op jit(solution)/shard_map/psum | solution.py:100
  354.9 13.2 %all-gather.8.cloned.1.call-done = bf16[16,256,128]{2,1,0:T(8,128)(2,1)} async-done(((bf16[4,256,128]{2,1,0:T(8,128)(2,1)}), bf16[16,256,128]{2,1,0:T(8,128)(2,1)}) %all-gather.8.cloned.1.call-update) | async-done | bytes 1048592 | tf_op jit(solution)/shard_map/all_gather | solution.py:86
  368.1 2.9 copy.42
  370.9 2.4 gather_fusion.4
  373.4 5.5 %all-to-all-start.5 = ((bf16[16,8,2,128]{3,0,2,1:T(8,128)(2,1)}), bf16[16,8,2,128]{3,0,2,1:T(8,128)(2,1)S(1)}, u32[]{:S(2)}, u32[]{:S(2)}) async-start(bf16[16,8,2,128]{3,0,2,1:T(8,128)(2,1)} %bitcast.30), calls=%async_computation.7 | async-start | bytes 131072 | tf_op jit(solution)/shard_map/all_to_all | solution.py:58
  378.9 8.0 %broadcast_select_fusion.4 = (f32[256,16,128]{2,1,0:T(8,128)}, f32[256,16,128]{2,1,0:T(8,128)}) fusion(pred[256]{0:T(512)(128)(4,1)S(1)} %fusion.43, bf16[256,1,128,128]{3,2,1,0:T(8,128)(2,1)} %param.7, bf16[16,256,128]{2,1,0:T(8,128)(2,1)} %all-gather.8.cloned.1.call-done), kind=kOutput, calls=%fused_computation.54 | convolution fusion | flops 134742016 | bytes 13631744 | tf_op jit(solution)/shard_map/rac,vra->vrc/dot_general | solution.py:63
  386.9 20.9 %scatter_fusion.7 = f32[16,17,128]{2,0,1:T(8,128)S(1)} fusion(f32[16,17,128]{2,0,1:T(8,128)S(1)} %broadcast.192, s32[256]{0:T(256)S(1)} %bitcast.118, f32[256,16,128]{2,1,0:T(8,128)} %get-tuple-element.215), kind=kCustom, calls=%fused_computation.14 | custom fusion | flops 524288 | bytes 6292480 | tf_op jit(solution)/shard_map/scatter-add | solution.py:69
  408.5 6.0 %all-to-all-start.6 = ((f32[16,8,2,128]{3,0,2,1:T(8,128)}), f32[16,8,2,128]{3,0,2,1:T(8,128)S(1)}, u32[]{:S(2)}, u32[]{:S(2)}) async-start(f32[16,8,2,128]{3,0,2,1:T(8,128)} %bitcast.34), calls=%async_computation.8 | async-start | bytes 262144 | tf_op jit(solution)/shard_map/all_to_all | solution.py:72
  414.7 2.3 pad_maximum_fusion.2
  417.1 3.0 gather_fusion.5
  420.1 9.5 %fusion.20 = f32[16,256,128]{2,0,1:T(8,128)} fusion(bf16[256,1,128,128]{3,2,1,0:T(8,128)(2,1)} %param.7, bf16[256,16,128]{2,1,0:T(8,128)(2,1)} %gather_fusion.5), kind=kOutput, calls=%fused_computation.38 | convolution fusion | flops 134217728 | bytes 11534336 | tf_op jit(solution)/shard_map/rac,vrc->vra/dot_general | solution.py:62
  429.6 31.4 %scatter_fusion.6 = f32[16,256,128]{2,0,1:T(8,128)} fusion(f32[16,256,128]{2,0,1:T(8,128)} %fusion.20, s32[256]{0:T(256)S(1)} %bitcast.114, f32[256,16,128]{2,1,0:T(8,128)} %get-tuple-element.214), kind=kCustom, calls=%fused_computation.13 | custom fusion | flops 524288 | bytes 6292480 | tf_op jit(solution)/shard_map/scatter-add | solution.py:65
  461.1 2.5 scatter_fusion.8
  463.7 3.1 fusion.28
  466.8 3.6 copy.45
  470.5 31.5 %reduce-scatter.8.cloned.1.call-done = f32[4,256,128]{2,1,0:T(8,128)} async-done(((f32[16,256,128]{2,1,0:T(8,128)}), f32[4,256,128]{2,1,0:T(8,128)}) %reduce-scatter.8.cloned.1.call-update) | async-done | bytes 524304 | tf_op jit(solution)/shard_map/reduce_scatter | solution.py:87
  503.4 21.3 %psum.31 = f32[4]{0:T(128)S(1)} all-reduce(f32[4]{0:T(128)S(1)} %multiply_reduce_fusion), channel_id=1, replica_groups=mesh['curve'=8,'band'=4] {'curve'}, use_global_device_ids=true, to_apply=%region_23.24 | all-reduce | flops 4 | bytes 32 | tf_op jit(solution)/shard_map/psum | solution.py:108
  525.9 2.1 multiply_add_fusion
  (84 shorter events, 22.9 us)
Async XLA Ops:
  6.5 113.7 %copy-start = (bf16[64,128,128]{2,1,0:T(8,128)(2,1)S(1)}, bf16[64,128,128]{2,1,0:T(8,128)(2,1)}, u32[]{:S(2)}) copy-start(bf16[64,128,128]{2,1,0:T(8,128)(2,1)} %param.8) | copy-start | bytes 6291460
  6.5 21.8 %all-gather.4.cloned.1.call-start = ((), (), s32[]{:S(2)}) async-start(), calls=%async_computation.10 | async-start | bytes 1310720 | tf_op jit(solution)/shard_map/all_gather | solution.py:86
  13.6 13.8 %all-to-all-start = ((s32[8,1,2]{2,1,0:T(1,128)}), s32[8,1,2]{2,1,0:T(1,128)S(1)}, u32[]{:S(2)}, u32[]{:S(2)}) async-start(s32[8,1,2]{2,1,0:T(1,128)} %bitcast.7), calls=%async_computation | async-start | bytes 8192 | tf_op jit(solution)/shard_map/all_to_all | solution.py:46
  31.4 35.1 %all-to-all-start.1 = ((bf16[16,8,2,128]{3,0,2,1:T(8,128)(2,1)}), bf16[16,8,2,128]{3,0,2,1:T(8,128)(2,1)S(1)}, u32[]{:S(2)}, u32[]{:S(2)}) async-start(bf16[16,8,2,128]{3,0,2,1:T(8,128)(2,1)} %bitcast.9), calls=%async_computation.1 | async-start | bytes 131072 | tf_op jit(solution)/shard_map/all_to_all | solution.py:58
  66.6 51.1 %all-to-all-start.2 = ((f32[16,8,2,128]{3,0,2,1:T(8,128)}), f32[16,8,2,128]{3,0,2,1:T(8,128)S(1)}, u32[]{:S(2)}, u32[]{:S(2)}) async-start(f32[16,8,2,128]{3,0,2,1:T(8,128)} %bitcast.16), calls=%async_computation.2 | async-start | bytes 262144 | tf_op jit(solution)/shard_map/all_to_all | solution.py:72
  72.6 86.2 %reduce-scatter.4.cloned.1.call-start = ((), (), s32[]{:S(2)}) async-start(), calls=%async_computation.11 | async-start | bytes 2621440 | tf_op jit(solution)/shard_map/reduce_scatter | solution.py:87
  126.9 31.8 %copy-start.2 = (f32[4,256,128]{2,1,0:T(8,128)S(1)}, f32[4,256,128]{2,1,0:T(8,128)}, u32[]{:S(2)}) copy-start(f32[4,256,128]{2,1,0:T(8,128)} %param.6) | copy-start | bytes 1572868
  127.0 69.5 %all-gather.6.cloned.1.call-start = ((), (), s32[]{:S(2)}) async-start(), calls=%async_computation.12 | async-start | bytes 1310720 | tf_op jit(solution)/shard_map/all_gather | solution.py:86
  201.7 35.1 %all-to-all-start.3 = ((bf16[16,8,2,128]{3,0,2,1:T(8,128)(2,1)}), bf16[16,8,2,128]{3,0,2,1:T(8,128)(2,1)S(1)}, u32[]{:S(2)}, u32[]{:S(2)}) async-start(bf16[16,8,2,128]{3,0,2,1:T(8,128)(2,1)} %bitcast.21), calls=%async_computation.4 | async-start | bytes 131072 | tf_op jit(solution)/shard_map/all_to_all | solution.py:58
  236.9 52.4 %all-to-all-start.4 = ((f32[16,8,2,128]{3,0,2,1:T(8,128)}), f32[16,8,2,128]{3,0,2,1:T(8,128)S(1)}, u32[]{:S(2)}, u32[]{:S(2)}) async-start(f32[16,8,2,128]{3,0,2,1:T(8,128)} %bitcast.25), calls=%async_computation.5 | async-start | bytes 262144 | tf_op jit(solution)/shard_map/all_to_all | solution.py:72
  242.9 87.5 %reduce-scatter.6.cloned.1.call-start = ((), (), s32[]{:S(2)}) async-start(), calls=%async_computation.13 | async-start | bytes 2621440 | tf_op jit(solution)/shard_map/reduce_scatter | solution.py:87
  298.6 69.5 %all-gather.8.cloned.1.call-start = ((), (), s32[]{:S(2)}) async-start(), calls=%async_computation.14 | async-start | bytes 1310720 | tf_op jit(solution)/shard_map/all_gather | solution.py:86
  373.4 35.1 %all-to-all-start.5 = ((bf16[16,8,2,128]{3,0,2,1:T(8,128)(2,1)}), bf16[16,8,2,128]{3,0,2,1:T(8,128)(2,1)S(1)}, u32[]{:S(2)}, u32[]{:S(2)}) async-start(bf16[16,8,2,128]{3,0,2,1:T(8,128)(2,1)} %bitcast.30), calls=%async_computation.7 | async-start | bytes 131072 | tf_op jit(solution)/shard_map/all_to_all | solution.py:58
  408.5 52.6 %all-to-all-start.6 = ((f32[16,8,2,128]{3,0,2,1:T(8,128)}), f32[16,8,2,128]{3,0,2,1:T(8,128)S(1)}, u32[]{:S(2)}, u32[]{:S(2)}) async-start(f32[16,8,2,128]{3,0,2,1:T(8,128)} %bitcast.34), calls=%async_computation.8 | async-start | bytes 262144 | tf_op jit(solution)/shard_map/all_to_all | solution.py:72
  414.5 87.5 %reduce-scatter.8.cloned.1.call-start = ((), (), s32[]{:S(2)}) async-start(), calls=%async_computation.15 | async-start | bytes 2621440 | tf_op jit(solution)/shard_map/reduce_scatter | solution.py:87
  470.4 31.6 %copy-start.1 = (f32[4,256,128]{2,1,0:T(8,128)S(1)}, f32[4,256,128]{2,1,0:T(8,128)}, u32[]{:S(2)}) copy-start(f32[4,256,128]{2,1,0:T(8,128)} %reduce-scatter.6.cloned.1.call-done) | copy-start | bytes 1572868
Sparse Core Ops, SparseCore 0:
  8.9 19.4 all-gather.3
  127.1 31.6 reduce-scatter.3
  183.4 12.9 all-gather.5
  298.7 31.6 reduce-scatter.5
  355.0 12.9 all-gather.7
  470.6 31.3 reduce-scatter.7
where the time goes:
time: 539 us; the launch traced here: 535 us
  other arithmetic  186 us (35%)
  waiting for transfers between devices  128 us (24%)
  blocking collectives  64 us (12%)
  matrix products  61.8 us (11%)
  starting transfers between devices  42.3 us (8%)
  local copies, waits for them, and re-layouts  38.1 us (7%)
  between operations  13.6 us (3%)
    reduce_scatter x3, waiting for transfers between devices, operate(): lax.psum_scatter(local_product(whole, blocks, diag_blocks, plan), 'band',...  95 us
    scatter-add x3, other arithmetic, local_product(): result = result.at[:, target, :].add(kept)  94.3 us
    scatter-add x3, other arithmetic, local_product(): outgoing = jnp.zeros((vectors, groups * CAP + 1, node_count), jnp.float32...  62.8 us
    dot_general x3, matrix products, local_product(): jnp.einsum('rac,vrc->vra', stored, gathered, preferred_element_type=jnp.f...  28.5 us
    all_gather x3, waiting for transfers between devices, operate(): whole = lax.all_gather(vector, 'band', axis=0, tiled=True)  27 us
    dot_general x3, matrix products, local_product(): jnp.einsum('rac,vra->vrc', stored, whole, preferred_element_type=jnp.floa...  24 us
    psum x1, blocking collectives, body(): lax.psum(jnp.sum(second * image_second, axis=(1, 2)), 'curve')  21.3 us
    psum x1, blocking collectives, body(): lax.psum((jnp.sum(first * image, axis=(1, 2)), jnp.sum(image * image, axi...  21.3 us
  transfers between devices with their start and end apart: 13, of which 7 were waited for; matrix products, arithmetic and copies ran while one was open for 43% of the time, Pallas kernels for 0%

commit v1 on v0

--- a/solution.py
+++ b/solution.py
@@ -83,7 +83,9 @@
 
 
 def operate(vector, blocks, diag_blocks, plan):
-    whole = lax.all_gather(vector, "band", axis=0, tiled=True)
+    whole = jnp.concatenate(
+        lax.all_to_all(jnp.stack([vector] * lax.axis_size("band")), "band", 0, 0), axis=0
+    )
     product = lax.psum_scatter(
         local_product(whole, blocks, diag_blocks, plan), "band", scatter_dimension=0, tiled=True
     )

time: 539 us -> 552 us (1.024)
  blocking collectives: 64 us -> 97.7 us
  waiting for transfers between devices: 128 us -> 114 us
    all_to_all x0 -> x2, blocking collectives: none -> 33.7 us  [operate(): lax.all_to_all(jnp.stack([vector] * lax.axis_size('band')), 'band', 0, 0)]
    all_gather x3 -> x0, waiting for transfers between devices: 27 us -> none  [operate(): whole = lax.all_gather(vector, 'band', axis=0, tiled=True)]
    all_to_all x0 -> x1, waiting for transfers between devices: none -> 14.2 us  [operate(): lax.all_to_all(jnp.stack([vector] * lax.axis_size('band')), 'band', 0, 0)]
    all_gather x3 -> x0, local copies, waits for them, and re-layouts: 7.66 us -> none  [operate(): whole = lax.all_gather(vector, 'band', axis=0, tiled=True)]
    all_to_all x3, starting transfers between devices: 16.5 us -> 10.2 us  [local_product(): lax.all_to_all(reply, 'curve', split_axis=1, concat_axis=1, tiled=True)]
  transfers between devices with their start and end apart: 13 -> 11, of which waited for: 7 -> 5; matrix products, arithmetic and copies ran while one was open for 43% -> 42% of each run, Pallas kernels for 0% -> 0%
where the time goes in v1:
time: 552 us; the launch traced here: 548 us
  other arithmetic  183 us (33%)
  waiting for transfers between devices  114 us (21%)
  blocking collectives  97.7 us (18%)
  matrix products  61.4 us (11%)
  starting transfers between devices  39.7 us (7%)
  local copies, waits for them, and re-layouts  37.2 us (7%)
  between operations  13.4 us (2%)
    reduce_scatter x3, waiting for transfers between devices, operate(): lax.psum_scatter(local_product(whole, blocks, diag_blocks, plan), 'band',...  94.6 us
    scatter-add x3, other arithmetic, local_product(): result = result.at[:, target, :].add(kept)  94.3 us
    scatter-add x3, other arithmetic, local_product(): outgoing = jnp.zeros((vectors, groups * CAP + 1, node_count), jnp.float32...  62.8 us
    all_to_all x2, blocking collectives, operate(): lax.all_to_all(jnp.stack([vector] * lax.axis_size('band')), 'band', 0, 0)  33.7 us
    dot_general x3, matrix products, local_product(): jnp.einsum('rac,vrc->vra', stored, gathered, preferred_element_type=jnp.f...  28.5 us
    dot_general x3, matrix products, local_product(): jnp.einsum('rac,vra->vrc', stored, whole, preferred_element_type=jnp.floa...  23.7 us
    psum x1, blocking collectives, body(): lax.psum((jnp.sum(first * image, axis=(1, 2)), jnp.sum(image * image, axi...  21.4 us
    psum x1, blocking collectives, body(): lax.psum(jnp.sum(second * image_second, axis=(1, 2)), 'curve')  21.3 us
  transfers between devices with their start and end apart: 11, of which 5 were waited for; matrix products, arithmetic and copies ran while one was open for 42% of the time, Pallas kernels for 0%

profile of v1, /device:TPU:0, one launch (start us, length us, event | category | flops | bytes accessed | tf_op | source)
XLA Modules:
  0.0 547.9 jit_solution(13934584730631738343)
XLA Ops:
  11.8 7.3 %all-to-all-start.1 = ((s32[8,1,2]{2,1,0:T(1,128)}), s32[8,1,2]{2,1,0:T(1,128)S(1)}, u32[]{:S(2)}, u32[]{:S(2)}) async-start(s32[8,1,2]{2,1,0:T(1,128)} %bitcast.8), calls=%async_computation.1 | async-start | bytes 8192 | tf_op jit(solution)/shard_map/all_to_all | solution.py:46
  20.4 5.1 all-to-all-done.1
  26.8 4.2 all-to-all-start
  31.4 14.2 %all-to-all-done = bf16[4,4,256,128]{3,1,2,0:T(4,128)(2,1)} async-done(((bf16[4,4,256,128]{3,1,2,0:T(4,128)(2,1)}), bf16[4,4,256,128]{3,1,2,0:T(4,128)(2,1)}, u32[]{:S(2)}, u32[]{:S(2)}) %all-to-all-start) | async-done | bytes 1048608 | tf_op jit(solution)/shard_map/all_to_all | solution.py:87
  45.6 1.6 copy.18
  48.4 3.3 all-to-all-start.2
  51.7 7.7 %broadcast_select_fusion.6 = (f32[256,16,128]{2,1,0:T(8,128)}, f32[256,16,128]{2,1,0:T(8,128)}) fusion(pred[256]{0:T(512)(128)(4,1)S(1)} %fusion.43, bf16[16,256,128]{2,0,1:T(8,128)(2,1)S(1)} %bitcast.113, bf16[256,1,128,128]{3,2,1,0:T(8,128)(2,1)} %param.7), kind=kOutput, calls=%fused_computation.56 | convolution fusion | flops 134742016 | bytes 13631744 | tf_op jit(solution)/shard_map/rac,vra->vrc/dot_general | solution.py:63
  59.4 20.9 %scatter_fusion.1 = f32[16,17,128]{2,0,1:T(8,128)S(1)} fusion(f32[16,17,128]{2,0,1:T(8,128)S(1)} %broadcast.198.clone, s32[256]{0:T(256)S(1)} %bitcast.134, f32[256,16,128]{2,1,0:T(8,128)} %get-tuple-element.211), kind=kCustom, calls=%fused_computation.8 | custom fusion | flops 524288 | bytes 6292480 | tf_op jit(solution)/shard_map/scatter-add | solution.py:69
  81.0 5.9 %all-to-all-start.3 = ((f32[16,8,2,128]{3,0,2,1:T(8,128)}), f32[16,8,2,128]{3,0,2,1:T(8,128)S(1)}, u32[]{:S(2)}, u32[]{:S(2)}) async-start(f32[16,8,2,128]{3,0,2,1:T(8,128)} %bitcast.17), calls=%async_computation.3 | async-start | bytes 262144 | tf_op jit(solution)/shard_map/all_to_all | solution.py:72
  88.1 3.0 gather_fusion.1
  91.1 9.5 %fusion.14 = f32[16,256,128]{2,0,1:T(8,128)} fusion(bf16[256,1,128,128]{3,2,1,0:T(8,128)(2,1)} %param.7, bf16[256,16,128]{2,1,0:T(8,128)(2,1)} %gather_fusion.1), kind=kOutput, calls=%fused_computation.36 | convolution fusion | flops 134217728 | bytes 11534336 | tf_op jit(solution)/shard_map/rac,vrc->vra/dot_general | solution.py:62
  100.6 31.4 %scatter_fusion = f32[16,256,128]{2,0,1:T(8,128)} fusion(f32[16,256,128]{2,0,1:T(8,128)} %fusion.14, s32[256]{0:T(256)S(1)} %bitcast.130, f32[256,16,128]{2,1,0:T(8,128)} %get-tuple-element.210), kind=kCustom, calls=%fused_computation.7 | custom fusion | flops 524288 | bytes 6292480 | tf_op jit(solution)/shard_map/scatter-add | solution.py:65
  132.1 2.5 scatter_fusion.2
  134.7 3.0 fusion.24
  137.7 3.6 copy.20
  141.3 31.6 %reduce-scatter.4.cloned.1.call-done = f32[4,256,128]{2,1,0:T(8,128)} async-done(((f32[16,256,128]{2,1,0:T(8,128)}), f32[4,256,128]{2,1,0:T(8,128)}) %reduce-scatter.4.cloned.1.call-update) | async-done | bytes 524304 | tf_op jit(solution)/shard_map/reduce_scatter | solution.py:89
  174.2 21.3 %psum.28 = f32[4]{0:T(128)S(1)} all-reduce(f32[4]{0:T(128)S(1)} %multiply_reduce_fusion.3), channel_id=1, replica_groups=mesh['curve'=8,'band'=4] {'curve'}, use_global_device_ids=true, to_apply=%region_9.10 | all-reduce | flops 4 | bytes 32 | tf_op jit(solution)/shard_map/psum | solution.py:98
  197.3 16.9 %all_to_all.54 = bf16[4,4,256,128]{3,1,2,0:T(4,128)(2,1)S(1)} all-to-all(bf16[4,4,256,128]{3,1,2,0:T(4,128)(2,1)S(1)} %stack.7), channel_id=1, replica_groups=mesh['curve'=8,'band'=4] {'band'}, dimensions={0} | all-to-all | bytes 2097152 | tf_op jit(solution)/shard_map/all_to_all | solution.py:87
  215.5 2.4 gather_fusion.2
  217.9 3.5 all-to-all-start.5
  221.4 8.0 %broadcast_select_fusion.5 = (f32[256,16,128]{2,1,0:T(8,128)}, f32[256,16,128]{2,1,0:T(8,128)}) fusion(pred[256]{0:T(512)(128)(4,1)S(1)} %fusion.43, bf16[16,256,128]{2,0,1:T(8,128)(2,1)} %bitcast.117, bf16[256,1,128,128]{3,2,1,0:T(8,128)(2,1)} %param.7), kind=kOutput, calls=%fused_computation.55 | convolution fusion | flops 134742016 | bytes 13631744 | tf_op jit(solution)/shard_map/rac,vra->vrc/dot_general | solution.py:63
  229.4 20.9 %scatter_fusion.4 = f32[16,17,128]{2,0,1:T(8,128)S(1)} fusion(f32[16,17,128]{2,0,1:T(8,128)S(1)} %broadcast.198.clone.1, s32[256]{0:T(256)S(1)} %bitcast.135, f32[256,16,128]{2,1,0:T(8,128)} %get-tuple-element.213), kind=kCustom, calls=%fused_computation.11 | custom fusion | flops 524288 | bytes 6292480 | tf_op jit(solution)/shard_map/scatter-add | solution.py:69
  251.0 5.8 %all-to-all-start.6 = ((f32[16,8,2,128]{3,0,2,1:T(8,128)}), f32[16,8,2,128]{3,0,2,1:T(8,128)S(1)}, u32[]{:S(2)}, u32[]{:S(2)}) async-start(f32[16,8,2,128]{3,0,2,1:T(8,128)} %bitcast.27), calls=%async_computation.7 | async-start | bytes 262144 | tf_op jit(solution)/shard_map/all_to_all | solution.py:72
  256.8 2.3 pad_maximum_fusion.1
  259.2 3.0 gather_fusion.3
  262.2 9.5 %fusion.17 = f32[16,256,128]{2,0,1:T(8,128)} fusion(bf16[256,1,128,128]{3,2,1,0:T(8,128)(2,1)} %param.7, bf16[256,16,128]{2,1,0:T(8,128)(2,1)} %gather_fusion.3), kind=kOutput, calls=%fused_computation.37 | convolution fusion | flops 134217728 | bytes 11534336 | tf_op jit(solution)/shard_map/rac,vrc->vra/dot_general | solution.py:62
  271.7 31.4 %scatter_fusion.3 = f32[16,256,128]{2,0,1:T(8,128)} fusion(f32[16,256,128]{2,0,1:T(8,128)} %fusion.17, s32[256]{0:T(256)S(1)} %bitcast.131, f32[256,16,128]{2,1,0:T(8,128)} %get-tuple-element.212), kind=kCustom, calls=%fused_computation.10 | custom fusion | flops 524288 | bytes 6292480 | tf_op jit(solution)/shard_map/scatter-add | solution.py:65
  303.2 2.5 scatter_fusion.5
  305.8 3.1 fusion.26
  308.9 3.6 copy.23
  312.5 31.6 %reduce-scatter.6.cloned.1.call-done = f32[4,256,128]{2,1,0:T(8,128)} async-done(((f32[16,256,128]{2,1,0:T(8,128)}), f32[4,256,128]{2,1,0:T(8,128)}) %reduce-scatter.6.cloned.1.call-update) | async-done | bytes 524304 | tf_op jit(solution)/shard_map/reduce_scatter | solution.py:89
  345.4 21.4 %all-reduce = (f32[4]{0:T(128)S(1)}, f32[4]{0:T(128)S(1)}) all-reduce(f32[4]{0:T(128)S(1)} %get-tuple-element.175, f32[4]{0:T(128)S(1)} %get-tuple-element.174), channel_id=1, replica_groups=mesh['curve'=8,'band'=4] {'curve'}, use_global_device_ids=true, to_apply=%region_15.16 | all-reduce | flops 8 | bytes 64 | tf_op jit(solution)/shard_map/psum | solution.py:102
  368.5 16.9 %all_to_all.55 = bf16[4,4,256,128]{3,1,2,0:T(4,128)(2,1)S(1)} all-to-all(bf16[4,4,256,128]{3,1,2,0:T(4,128)(2,1)S(1)} %stack.8), channel_id=1, replica_groups=mesh['curve'=8,'band'=4] {'band'}, dimensions={0} | all-to-all | bytes 2097152 | tf_op jit(solution)/shard_map/all_to_all | solution.py:87
  386.7 2.4 gather_fusion.4
  389.1 3.3 all-to-all-start.8
  392.4 8.0 %broadcast_select_fusion.4 = (f32[256,16,128]{2,1,0:T(8,128)}, f32[256,16,128]{2,1,0:T(8,128)}) fusion(pred[256]{0:T(512)(128)(4,1)S(1)} %fusion.43, bf16[16,256,128]{2,0,1:T(8,128)(2,1)} %bitcast.109, bf16[256,1,128,128]{3,2,1,0:T(8,128)(2,1)} %param.7), kind=kOutput, calls=%fused_computation.54 | convolution fusion | flops 134742016 | bytes 13631744 | tf_op jit(solution)/shard_map/rac,vra->vrc/dot_general | solution.py:63
  400.4 20.9 %scatter_fusion.7 = f32[16,17,128]{2,0,1:T(8,128)S(1)} fusion(f32[16,17,128]{2,0,1:T(8,128)S(1)} %broadcast.198, s32[256]{0:T(256)S(1)} %bitcast.136, f32[256,16,128]{2,1,0:T(8,128)} %get-tuple-element.215), kind=kCustom, calls=%fused_computation.14 | custom fusion | flops 524288 | bytes 6292480 | tf_op jit(solution)/shard_map/scatter-add | solution.py:69
  422.0 5.9 %all-to-all-start.9 = ((f32[16,8,2,128]{3,0,2,1:T(8,128)}), f32[16,8,2,128]{3,0,2,1:T(8,128)S(1)}, u32[]{:S(2)}, u32[]{:S(2)}) async-start(f32[16,8,2,128]{3,0,2,1:T(8,128)} %bitcast.37), calls=%async_computation.11 | async-start | bytes 262144 | tf_op jit(solution)/shard_map/all_to_all | solution.py:72
  428.2 2.3 pad_maximum_fusion.2
  430.6 3.0 gather_fusion.5
  433.6 9.5 %fusion.20 = f32[16,256,128]{2,0,1:T(8,128)} fusion(bf16[256,1,128,128]{3,2,1,0:T(8,128)(2,1)} %param.7, bf16[256,16,128]{2,1,0:T(8,128)(2,1)} %gather_fusion.5), kind=kOutput, calls=%fused_computation.38 | convolution fusion | flops 134217728 | bytes 11534336 | tf_op jit(solution)/shard_map/rac,vrc->vra/dot_general | solution.py:62
  443.1 31.4 %scatter_fusion.6 = f32[16,256,128]{2,0,1:T(8,128)} fusion(f32[16,256,128]{2,0,1:T(8,128)} %fusion.20, s32[256]{0:T(256)S(1)} %bitcast.132, f32[256,16,128]{2,1,0:T(8,128)} %get-tuple-element.214), kind=kCustom, calls=%fused_computation.13 | custom fusion | flops 524288 | bytes 6292480 | tf_op jit(solution)/shard_map/scatter-add | solution.py:65
  474.6 2.5 scatter_fusion.8
  477.2 3.1 fusion.28
  480.3 3.6 copy.26
  484.0 31.4 %reduce-scatter.8.cloned.1.call-done = f32[4,256,128]{2,1,0:T(8,128)} async-done(((f32[16,256,128]{2,1,0:T(8,128)}), f32[4,256,128]{2,1,0:T(8,128)}) %reduce-scatter.8.cloned.1.call-update) | async-done | bytes 524304 | tf_op jit(solution)/shard_map/reduce_scatter | solution.py:89
  516.7 21.3 %psum.31 = f32[4]{0:T(128)S(1)} all-reduce(f32[4]{0:T(128)S(1)} %multiply_reduce_fusion), channel_id=1, replica_groups=mesh['curve'=8,'band'=4] {'curve'}, use_global_device_ids=true, to_apply=%region_23.24 | all-reduce | flops 4 | bytes 32 | tf_op jit(solution)/shard_map/psum | solution.py:110
  539.3 2.1 multiply_add_fusion
  (87 shorter events, 24.5 us)
Async XLA Ops:
  6.5 128.1 %copy-start = (bf16[64,128,128]{2,1,0:T(8,128)(2,1)S(1)}, bf16[64,128,128]{2,1,0:T(8,128)(2,1)}, u32[]{:S(2)}) copy-start(bf16[64,128,128]{2,1,0:T(8,128)(2,1)} %param.8) | copy-start | bytes 6291460
  11.8 13.7 %all-to-all-start.1 = ((s32[8,1,2]{2,1,0:T(1,128)}), s32[8,1,2]{2,1,0:T(1,128)S(1)}, u32[]{:S(2)}, u32[]{:S(2)}) async-start(s32[8,1,2]{2,1,0:T(1,128)} %bitcast.8), calls=%async_computation.1 | async-start | bytes 8192 | tf_op jit(solution)/shard_map/all_to_all | solution.py:46
  20.2 10.9 %copy-start.3 = (s32[256,1]{0,1:T(1,128)S(1)}, s32[256,1]{0,1:T(1,128)}, u32[]{:S(2)}) copy-start(s32[256,1]{0,1:T(1,128)} %param.9) | copy-start | bytes 3076
  26.8 18.7 %all-to-all-start = ((bf16[4,4,256,128]{3,1,2,0:T(4,128)(2,1)}), bf16[4,4,256,128]{3,1,2,0:T(4,128)(2,1)}, u32[]{:S(2)}, u32[]{:S(2)}) async-start(bf16[4,4,256,128]{3,1,2,0:T(4,128)(2,1)} %stack.6), calls=%async_computation | async-start | bytes 2097152 | tf_op jit(solution)/shard_map/all_to_all | solution.py:87
  48.4 32.6 %all-to-all-start.2 = ((bf16[16,8,2,128]{3,0,2,1:T(8,128)(2,1)}), bf16[16,8,2,128]{3,0,2,1:T(8,128)(2,1)S(1)}, u32[]{:S(2)}, u32[]{:S(2)}) async-start(bf16[16,8,2,128]{3,0,2,1:T(8,128)(2,1)} %bitcast.10), calls=%async_computation.2 | async-start | bytes 131072 | tf_op jit(solution)/shard_map/all_to_all | solution.py:58
  81.0 51.0 %all-to-all-start.3 = ((f32[16,8,2,128]{3,0,2,1:T(8,128)}), f32[16,8,2,128]{3,0,2,1:T(8,128)S(1)}, u32[]{:S(2)}, u32[]{:S(2)}) async-start(f32[16,8,2,128]{3,0,2,1:T(8,128)} %bitcast.17), calls=%async_computation.3 | async-start | bytes 262144 | tf_op jit(solution)/shard_map/all_to_all | solution.py:72
  86.9 86.1 %reduce-scatter.4.cloned.1.call-start = ((), (), s32[]{:S(2)}) async-start(), calls=%async_computation.13 | async-start | bytes 2621440 | tf_op jit(solution)/shard_map/reduce_scatter | solution.py:89
  141.3 31.7 %copy-start.2 = (f32[4,256,128]{2,1,0:T(8,128)S(1)}, f32[4,256,128]{2,1,0:T(8,128)}, u32[]{:S(2)}) copy-start(f32[4,256,128]{2,1,0:T(8,128)} %param.6) | copy-start | bytes 1572868
  217.9 33.1 %all-to-all-start.5 = ((bf16[16,8,2,128]{3,0,2,1:T(8,128)(2,1)}), bf16[16,8,2,128]{3,0,2,1:T(8,128)(2,1)S(1)}, u32[]{:S(2)}, u32[]{:S(2)}) async-start(bf16[16,8,2,128]{3,0,2,1:T(8,128)(2,1)} %bitcast.23), calls=%async_computation.6 | async-start | bytes 131072 | tf_op jit(solution)/shard_map/all_to_all | solution.py:58
  251.0 52.1 %all-to-all-start.6 = ((f32[16,8,2,128]{3,0,2,1:T(8,128)}), f32[16,8,2,128]{3,0,2,1:T(8,128)S(1)}, u32[]{:S(2)}, u32[]{:S(2)}) async-start(f32[16,8,2,128]{3,0,2,1:T(8,128)} %bitcast.27), calls=%async_computation.7 | async-start | bytes 262144 | tf_op jit(solution)/shard_map/all_to_all | solution.py:72
  256.8 87.4 %reduce-scatter.6.cloned.1.call-start = ((), (), s32[]{:S(2)}) async-start(), calls=%async_computation.14 | async-start | bytes 2621440 | tf_op jit(solution)/shard_map/reduce_scatter | solution.py:89
  389.1 33.0 %all-to-all-start.8 = ((bf16[16,8,2,128]{3,0,2,1:T(8,128)(2,1)}), bf16[16,8,2,128]{3,0,2,1:T(8,128)(2,1)S(1)}, u32[]{:S(2)}, u32[]{:S(2)}) async-start(bf16[16,8,2,128]{3,0,2,1:T(8,128)(2,1)} %bitcast.33), calls=%async_computation.10 | async-start | bytes 131072 | tf_op jit(solution)/shard_map/all_to_all | solution.py:58
  422.0 52.5 %all-to-all-start.9 = ((f32[16,8,2,128]{3,0,2,1:T(8,128)}), f32[16,8,2,128]{3,0,2,1:T(8,128)S(1)}, u32[]{:S(2)}, u32[]{:S(2)}) async-start(f32[16,8,2,128]{3,0,2,1:T(8,128)} %bitcast.37), calls=%async_computation.11 | async-start | bytes 262144 | tf_op jit(solution)/shard_map/all_to_all | solution.py:72
  428.0 87.4 %reduce-scatter.8.cloned.1.call-start = ((), (), s32[]{:S(2)}) async-start(), calls=%async_computation.15 | async-start | bytes 2621440 | tf_op jit(solution)/shard_map/reduce_scatter | solution.py:89
  483.9 31.4 %copy-start.1 = (f32[4,256,128]{2,1,0:T(8,128)S(1)}, f32[4,256,128]{2,1,0:T(8,128)}, u32[]{:S(2)}) copy-start(f32[4,256,128]{2,1,0:T(8,128)} %reduce-scatter.6.cloned.1.call-done) | copy-start | bytes 1572868
Sparse Core Ops, SparseCore 0:
  141.5 31.4 reduce-scatter.3
  312.7 31.4 reduce-scatter.5
  484.1 31.2 reduce-scatter.7
